TPU v7x, 32 devices: a whole 2x2x4 slice. The times are simulated.
32 devices in a mesh: grp: 2 (over y), tile: 4 (over z), sub: 4 (over x, core).
Axes of the slice: x: 2, y: 2, z: 4, core: 2. Of those that a mesh axis runs over, the one named last changes fastest.
Arguments:
- features: bfloat16 [24, 32, 1024], P(('grp', 'tile'), 'sub'), parts along dimension 0, may hold values from -6 to 6
- out_grad: bfloat16 [24, 32, 1024], P(('grp', 'tile'), 'sub'), parts along dimension 0, may hold values from -6 to 6
- filters: bfloat16 [5, 32, 32], replicated, may hold values from -0.5 to 0.5
- tile_map: int32 [12], replicated, may hold values from 0 to 11, as said below
Outputs:
- in_grad: bfloat16 [24, 32, 1024], P(('grp', 'tile'), 'sub'), parts along dimension 0
- weight_grad: float32 [10, 32, 32], P('grp', 'sub'), parts along dimension 0
There are 2 independent parts, one for each index of `grp`. A program takes and returns all parts, laid end to end along the dimension named above; an argument that names none is the same for every part. Nothing has to cross between parts.
Inputs may be any that keep to these rules, and one draw needn't show every extreme that they name: tile_map[s] is the nested index of the tile held in slot s; slots 3 * j to 3 * j + 2 lie on index j of tile and hold the nested indices 3 * j to 3 * j + 2 in some order.
All inputs are finite; a program needn't handle non-finite values.
Results may differ from a plain program's by a relative error of at most 0.00045.
Values may be sent and summed in bfloat16 or wider, within the bound.
No kernel may reach another device: no remote copies, remote signals or barrier semaphores. Data moves between devices by JAX's collectives and lax.ppermute only.
A program may use at most 64 MiB of HBM per device.

v0:
```python
import math
import jax
import jax.numpy as jnp
import numpy as np
from jax import lax
from jax.sharding import PartitionSpec as P

K = 5


def from_behind(value, axis, steps):
    count = lax.axis_size(axis)
    pairs = [(source, (source + steps) % count) for source in range(count)]
    return lax.ppermute(value, axis, pairs)


def tile_coords(nested_code, bit_count):
    coord_x = nested_code * 0
    coord_y = nested_code * 0
    for bit_level in range(bit_count):
        coord_x = coord_x + nested_code // 4**bit_level % 2 * 2**bit_level
        coord_y = coord_y + nested_code // (2 * 4**bit_level) % 2 * 2**bit_level
    return (coord_x, coord_y)


def nested_index(coord_x, coord_y, bit_count):
    nested_code = coord_x * 0
    for bit_level in range(bit_count):
        nested_code = nested_code + coord_x // 2**bit_level % 2 * 4**bit_level
        nested_code = nested_code + coord_y // 2**bit_level % 2 * (2 * 4**bit_level)
    return nested_code


def pick(condition, when_true, when_false):
    return when_false + (when_true - when_false) * condition


def neighbour_codes(tile_ids, per_face, side_count):
    bit_count = side_count.bit_length() - 1
    face_id = tile_ids // per_face
    coord_x, coord_y = tile_coords(tile_ids % per_face, bit_count)
    column = face_id % 4
    is_north = face_id < 4
    is_south = face_id >= 8
    last_tile = side_count - 1

    def by_cycle(north_value, equator_value, south_value):
        return pick(is_north, north_value, pick(is_south, south_value, equator_value))

    side_rules = [
        (
            coord_x > 0,
            (face_id, coord_x - 1, coord_y, 1),
            (
                by_cycle(4 + column, 8 + (column + 3) % 4, 8 + (column + 3) % 4),
                by_cycle(last_tile, last_tile, coord_y),
                by_cycle(coord_y, coord_y, 0),
                by_cycle(1, 1, 2),
            ),
        ),
        (
            coord_x < last_tile,
            (face_id, coord_x + 1, coord_y, 0),
            (
                by_cycle((column + 1) % 4, column, 4 + (column + 1) % 4),
                by_cycle(coord_y, 0, 0),
                by_cycle(last_tile, coord_y, coord_y),
                by_cycle(3, 0, 0),
            ),
        ),
        (
            coord_y > 0,
            (face_id, coord_x, coord_y - 1, 3),
            (
                by_cycle(4 + (column + 1) % 4, 8 + column, 8 + (column + 1) % 4),
                by_cycle(coord_x, coord_x, 0),
                by_cycle(last_tile, last_tile, coord_x),
                by_cycle(3, 3, 0),
            ),
        ),
        (
            coord_y < last_tile,
            (face_id, coord_x, coord_y + 1, 2),
            (
                by_cycle((column + 3) % 4, (column + 3) % 4, 4 + column),
                by_cycle(last_tile, coord_x, coord_x),
                by_cycle(coord_x, 0, 0),
                by_cycle(1, 2, 2),
            ),
        ),
    ]
    target_list = []
    edge_list = []
    for inside, within, across in side_rules:
        chosen = [
            pick(inside, near_value, far_value) for near_value, far_value in zip(within, across)
        ]
        target_list.append(chosen[0] * per_face + nested_index(chosen[1], chosen[2], bit_count))
        edge_list.append(chosen[3] + tile_ids * 0)
    return (target_list, edge_list)


def neighbour_table(tile_map, per_face, side_count):
    target_list, edge_list = neighbour_codes(tile_map, per_face, side_count)
    targets = jnp.stack(target_list, axis=1).astype(jnp.int32)
    edges = jnp.stack(edge_list, axis=1).astype(jnp.int32)
    slot_of = jnp.argsort(tile_map).astype(jnp.int32)
    return (slot_of[targets].astype(jnp.int32), edges)


def peer_offsets(slot_count, device_count, per_face, side_count):
    tile_ids = np.arange(slot_count * device_count, dtype=np.int64)
    target_list, edge_list = neighbour_codes(tile_ids, per_face, side_count)
    targets = np.stack(target_list, axis=1)
    offsets = (tile_ids[:, None] // slot_count - targets // slot_count) % device_count
    distinct = sorted(set((int(value) for value in offsets.ravel())) - {0})
    position = np.zeros(device_count, dtype=np.int32)
    for order, value in enumerate(distinct):
        position[value] = order + 1
    return (distinct, position)


def edge_lines(values, tile_side):
    return jnp.stack(
        [
            values[..., :tile_side],
            values[..., -tile_side:],
            values[..., ::tile_side],
            values[..., tile_side - 1 :: tile_side],
        ],
        axis=1,
    )


def stencil(values, ghosts, tile_side):
    position = jnp.arange(values.shape[-1]) % tile_side
    zero_line = jnp.zeros_like(values[..., :1])
    upper_side = jnp.concatenate([ghosts[:, 0], values[..., :-tile_side]], axis=-1)
    lower_side = jnp.concatenate([values[..., tile_side:], ghosts[:, 1]], axis=-1)
    left_side = jnp.where(
        position == 0,
        jnp.repeat(ghosts[:, 2], tile_side, axis=-1),
        jnp.concatenate([zero_line, values[..., :-1]], axis=-1),
    )
    right_side = jnp.where(
        position == tile_side - 1,
        jnp.repeat(ghosts[:, 3], tile_side, axis=-1),
        jnp.concatenate([values[..., 1:], zero_line], axis=-1),
    )
    return -0.25 * (upper_side + lower_side + left_side + right_side)


def tile_total(filter_part):
    return lax.psum(filter_part, "tile")


def on_device(features, out_grad, filters, tile_map):
    slot_count = features.shape[0]
    group_channels = features.shape[1]
    tile_side = math.isqrt(features.shape[2])
    device_count = lax.axis_size("tile")
    total_tiles = slot_count * device_count
    side_count = math.isqrt(total_tiles // 12)
    scale_factor = 1.0 / math.sqrt(total_tiles * features.shape[2])
    highest = lax.Precision.HIGHEST
    slot_table, edge_table = neighbour_table(tile_map, total_tiles // 12, side_count)
    my_device = lax.axis_index("tile")
    first_slot = my_device * slot_count
    my_slots = lax.dynamic_slice_in_dim(slot_table, first_slot, slot_count, 0)
    my_edges = lax.dynamic_slice_in_dim(edge_table, first_slot, slot_count, 0)
    channel_start = lax.axis_index("sub") * group_channels
    weights = filters.astype(jnp.float32)
    distinct, position = peer_offsets(slot_count, device_count, total_tiles // 12, side_count)
    sender_gap = (my_device - my_slots // slot_count) % device_count
    local_rows = jnp.asarray(position)[sender_gap] * slot_count + my_slots % slot_count

    def laplace(values):
        border = edge_lines(values, tile_side).reshape(slot_count, 4, group_channels * tile_side)
        received = [border]
        for offset_value in distinct:
            received.append(from_behind(border, "tile", offset_value))
        stacked = jnp.concatenate(received, axis=0)
        stacked = stacked.reshape(stacked.shape[0], 4, group_channels, tile_side)
        ghosts = stacked[local_rows, my_edges]
        return stencil(values, ghosts, tile_side)

    whole_grad = lax.all_gather(out_grad, "sub", axis=1, tiled=True)
    cotangent = whole_grad.astype(jnp.float32)
    inputs = features.astype(jnp.float32)
    previous, current = (inputs, laplace(inputs))
    filter_terms = [
        jnp.einsum("sip,sop->io", inputs, cotangent, precision=highest),
        jnp.einsum("sip,sop->io", current, cotangent, precision=highest),
    ]
    for degree in range(2, K):
        previous, current = (current, 2.0 * laplace(current) - previous)
        filter_terms.append(jnp.einsum("sip,sop->io", current, cotangent, precision=highest))
    weight_grad = tile_total(jnp.stack(filter_terms)) * scale_factor
    row_block = lax.dynamic_slice_in_dim(weights, channel_start, group_channels, 1)

    def mixed(degree):
        return jnp.einsum("sop,io->sip", cotangent, row_block[degree], precision=highest)

    next_sum = mixed(K - 1)
    after_next = jnp.zeros_like(next_sum)
    for degree in range(K - 2, 0, -1):
        next_sum, after_next = (mixed(degree) + 2.0 * laplace(next_sum) - after_next, next_sum)
    in_grad = (mixed(0) + laplace(next_sum) - after_next).astype(jnp.bfloat16)
    return (in_grad, weight_grad)


def solution(mesh):
    placed = (P(("grp", "tile"), "sub", None), P(("grp", "tile"), "sub", None), P(), P())
    return jax.shard_map(
        on_device,
        mesh=mesh,
        in_specs=placed,
        out_specs=(P(("grp", "tile"), "sub", None), P("grp", "sub", None)),
        check_vma=False,
    )
```

profile of v0, /device:TPU:0, one launch (start us, length us, event | category | flops | bytes accessed | tf_op | source)
XLA Modules:
  0.0 89.9 jit_solution(3915343842741492382)
XLA Ops:
  0.7 0.8 fusion.100
  2.1 3.1 %collective-permute-start.12 = (f32[3,4,256]{2,0,1:T(4,128)S(1)}, f32[3,4,256]{2,0,1:T(4,128)S(1)}, u32[]{:S(2)}, u32[]{:S(2)}) collective-permute-start(f32[3,4,256]{2,0,1:T(4,128)S(1)} %constant_dynamic-update-slice_fusion.16), channel_id=1, source_target_pairs={{0,4},{4,8},{8,12},{12,0},{1,5},{5,9},{9,13},{13,1},{2,6},{6,10},{... | collective-permute-start | bytes 36872 | tf_op jit(solution)/shard_map/ppermute | solution.py:14
  5.2 2.6 %collective-permute-start.13 = (f32[3,4,256]{2,0,1:T(4,128)S(1)}, f32[3,4,256]{2,0,1:T(4,128)S(1)}, u32[]{:S(2)}, u32[]{:S(2)}) collective-permute-start(f32[3,4,256]{2,0,1:T(4,128)S(1)} %constant_dynamic-update-slice_fusion.16), channel_id=1, source_target_pairs={{0,8},{4,12},{8,0},{12,4},{1,9},{5,13},{9,1},{13,5},{2,10},{6,14},... | collective-permute-start | bytes 36872 | tf_op jit(solution)/shard_map/ppermute | solution.py:14
  7.8 1.3 %collective-permute-start.14 = (f32[3,4,256]{2,0,1:T(4,128)S(1)}, f32[3,4,256]{2,0,1:T(4,128)S(1)}, u32[]{:S(2)}, u32[]{:S(2)}) collective-permute-start(f32[3,4,256]{2,0,1:T(4,128)S(1)} %constant_dynamic-update-slice_fusion.16), channel_id=1, source_target_pairs={{0,12},{4,0},{8,4},{12,8},{1,13},{5,1},{9,5},{13,9},{2,14},{6,2},{... | collective-permute-start | bytes 36872 | tf_op jit(solution)/shard_map/ppermute | solution.py:14
  9.2 5.6 %all_gather.3 = bf16[3,32,1024]{2,1,0:T(8,128)(2,1)S(1)} all-gather(bf16[3,8,1024]{2,1,0:T(8,128)(2,1)S(1)} %copy-done.2), channel_id=1, replica_groups=mesh['grp'=2,'tile'=4,'sub'=4] {'sub'}, dimensions={1}, use_global_device_ids=true | all-gather | bytes 245760 | tf_op jit(solution)/shard_map/all_gather | solution.py:187
  15.7 0.7 collective-permute-start
  18.3 1.2 %sort.17 = (s32[12]{0:T(128)}, s32[12]{0:T(128)S(1)}) sort(s32[12]{0:T(128)S(1)} %copy-done.3, s32[12]{0:T(128)S(1)} %iota.45), dimensions={0}, to_apply=%region_0.1 | sort | flops 48 | bytes 192 | tf_op jit(solution)/shard_map/jit(argsort)/sort | solution.py:107
  19.6 0.8 gather_fusion
  21.4 2.8 %collective-permute-start.2 = (f32[3,4,256]{2,0,1:T(4,128)S(1)}, f32[3,4,256]{2,0,1:T(4,128)S(1)}, u32[]{:S(2)}, u32[]{:S(2)}) collective-permute-start(f32[3,4,256]{2,0,1:T(4,128)S(1)} %constant_dynamic-update-slice_fusion), channel_id=1, source_target_pairs={{0,12},{4,0},{8,4},{12,8},{1,13},{5,1},{9,5},{13,9},{2,14},{6,2},{... | collective-permute-start | bytes 36872 | tf_op jit(solution)/shard_map/ppermute | solution.py:14
  27.3 1.5 %collective-permute-start.16 = (f32[3,4,256]{2,0,1:T(4,128)S(1)}, f32[3,4,256]{2,0,1:T(4,128)S(1)}, u32[]{:S(2)}, u32[]{:S(2)}) collective-permute-start(f32[3,4,256]{2,0,1:T(4,128)S(1)} %constant_dynamic-update-slice_fusion.20), channel_id=1, source_target_pairs={{0,8},{4,12},{8,0},{12,4},{1,9},{5,13},{9,1},{13,5},{2,10},{6,14},... | collective-permute-start | bytes 36872 | tf_op jit(solution)/shard_map/ppermute | solution.py:14
  29.0 2.9 %collective-permute-start.17 = (f32[3,4,256]{2,0,1:T(4,128)S(1)}, f32[3,4,256]{2,0,1:T(4,128)S(1)}, u32[]{:S(2)}, u32[]{:S(2)}) collective-permute-start(f32[3,4,256]{2,0,1:T(4,128)S(1)} %constant_dynamic-update-slice_fusion.20), channel_id=1, source_target_pairs={{0,12},{4,0},{8,4},{12,8},{1,13},{5,1},{9,5},{13,9},{2,14},{6,2},{... | collective-permute-start | bytes 36872 | tf_op jit(solution)/shard_map/ppermute | solution.py:14
  34.4 1.0 %collective-permute-start.4 = (f32[3,4,256]{2,0,1:T(4,128)S(1)}, f32[3,4,256]{2,0,1:T(4,128)S(1)}, u32[]{:S(2)}, u32[]{:S(2)}) collective-permute-start(f32[3,4,256]{2,0,1:T(4,128)S(1)} %constant_dynamic-update-slice_fusion.4), channel_id=1, source_target_pairs={{0,8},{4,12},{8,0},{12,4},{1,9},{5,13},{9,1},{13,5},{2,10},{6,14},... | collective-permute-start | bytes 36872 | tf_op jit(solution)/shard_map/ppermute | solution.py:14
  35.8 2.9 %collective-permute-start.5 = (f32[3,4,256]{2,0,1:T(4,128)S(1)}, f32[3,4,256]{2,0,1:T(4,128)S(1)}, u32[]{:S(2)}, u32[]{:S(2)}) collective-permute-start(f32[3,4,256]{2,0,1:T(4,128)S(1)} %constant_dynamic-update-slice_fusion.4), channel_id=1, source_target_pairs={{0,12},{4,0},{8,4},{12,8},{1,13},{5,1},{9,5},{13,9},{2,14},{6,2},{... | collective-permute-start | bytes 36872 | tf_op jit(solution)/shard_map/ppermute | solution.py:14
  41.8 1.5 %collective-permute-start.19 = (f32[3,4,256]{2,0,1:T(4,128)S(1)}, f32[3,4,256]{2,0,1:T(4,128)S(1)}, u32[]{:S(2)}, u32[]{:S(2)}) collective-permute-start(f32[3,4,256]{2,0,1:T(4,128)S(1)} %constant_dynamic-update-slice_fusion.24), channel_id=1, source_target_pairs={{0,8},{4,12},{8,0},{12,4},{1,9},{5,13},{9,1},{13,5},{2,10},{6,14},... | collective-permute-start | bytes 36872 | tf_op jit(solution)/shard_map/ppermute | solution.py:14
  43.5 2.9 %collective-permute-start.20 = (f32[3,4,256]{2,0,1:T(4,128)S(1)}, f32[3,4,256]{2,0,1:T(4,128)S(1)}, u32[]{:S(2)}, u32[]{:S(2)}) collective-permute-start(f32[3,4,256]{2,0,1:T(4,128)S(1)} %constant_dynamic-update-slice_fusion.24), channel_id=1, source_target_pairs={{0,12},{4,0},{8,4},{12,8},{1,13},{5,1},{9,5},{13,9},{2,14},{6,2},{... | collective-permute-start | bytes 36872 | tf_op jit(solution)/shard_map/ppermute | solution.py:14
  48.9 1.0 %collective-permute-start.7 = (f32[3,4,256]{2,0,1:T(4,128)S(1)}, f32[3,4,256]{2,0,1:T(4,128)S(1)}, u32[]{:S(2)}, u32[]{:S(2)}) collective-permute-start(f32[3,4,256]{2,0,1:T(4,128)S(1)} %constant_dynamic-update-slice_fusion.8), channel_id=1, source_target_pairs={{0,8},{4,12},{8,0},{12,4},{1,9},{5,13},{9,1},{13,5},{2,10},{6,14},... | collective-permute-start | bytes 36872 | tf_op jit(solution)/shard_map/ppermute | solution.py:14
  50.3 2.9 %collective-permute-start.8 = (f32[3,4,256]{2,0,1:T(4,128)S(1)}, f32[3,4,256]{2,0,1:T(4,128)S(1)}, u32[]{:S(2)}, u32[]{:S(2)}) collective-permute-start(f32[3,4,256]{2,0,1:T(4,128)S(1)} %constant_dynamic-update-slice_fusion.8), channel_id=1, source_target_pairs={{0,12},{4,0},{8,4},{12,8},{1,13},{5,1},{9,5},{13,9},{2,14},{6,2},{... | collective-permute-start | bytes 36872 | tf_op jit(solution)/shard_map/ppermute | solution.py:14
  56.3 1.5 %collective-permute-start.22 = (f32[3,4,256]{2,0,1:T(4,128)S(1)}, f32[3,4,256]{2,0,1:T(4,128)S(1)}, u32[]{:S(2)}, u32[]{:S(2)}) collective-permute-start(f32[3,4,256]{2,0,1:T(4,128)S(1)} %constant_dynamic-update-slice_fusion.28), channel_id=1, source_target_pairs={{0,8},{4,12},{8,0},{12,4},{1,9},{5,13},{9,1},{13,5},{2,10},{6,14},... | collective-permute-start | bytes 36872 | tf_op jit(solution)/shard_map/ppermute | solution.py:14
  58.0 2.9 %collective-permute-start.23 = (f32[3,4,256]{2,0,1:T(4,128)S(1)}, f32[3,4,256]{2,0,1:T(4,128)S(1)}, u32[]{:S(2)}, u32[]{:S(2)}) collective-permute-start(f32[3,4,256]{2,0,1:T(4,128)S(1)} %constant_dynamic-update-slice_fusion.28), channel_id=1, source_target_pairs={{0,12},{4,0},{8,4},{12,8},{1,13},{5,1},{9,5},{13,9},{2,14},{6,2},{... | collective-permute-start | bytes 36872 | tf_op jit(solution)/shard_map/ppermute | solution.py:14
  63.3 1.0 %collective-permute-start.10 = (f32[3,4,256]{2,0,1:T(4,128)S(1)}, f32[3,4,256]{2,0,1:T(4,128)S(1)}, u32[]{:S(2)}, u32[]{:S(2)}) collective-permute-start(f32[3,4,256]{2,0,1:T(4,128)S(1)} %constant_dynamic-update-slice_fusion.12), channel_id=1, source_target_pairs={{0,8},{4,12},{8,0},{12,4},{1,9},{5,13},{9,1},{13,5},{2,10},{6,14},... | collective-permute-start | bytes 36872 | tf_op jit(solution)/shard_map/ppermute | solution.py:14
  64.3 0.9 %collective-permute-start.11 = (f32[3,4,256]{2,0,1:T(4,128)S(1)}, f32[3,4,256]{2,0,1:T(4,128)S(1)}, u32[]{:S(2)}, u32[]{:S(2)}) collective-permute-start(f32[3,4,256]{2,0,1:T(4,128)S(1)} %constant_dynamic-update-slice_fusion.12), channel_id=1, source_target_pairs={{0,12},{4,0},{8,4},{12,8},{1,13},{5,1},{9,5},{13,9},{2,14},{6,2},{... | collective-permute-start | bytes 36872 | tf_op jit(solution)/shard_map/ppermute | solution.py:14
  65.7 1.1 %collective-permute-start.9 = (f32[3,4,256]{2,0,1:T(4,128)S(1)}, f32[3,4,256]{2,0,1:T(4,128)S(1)}, u32[]{:S(2)}, u32[]{:S(2)}) collective-permute-start(f32[3,4,256]{2,0,1:T(4,128)S(1)} %constant_dynamic-update-slice_fusion.12), channel_id=1, source_target_pairs={{0,4},{4,8},{8,12},{12,0},{1,5},{5,9},{9,13},{13,1},{2,6},{6,10},{... | collective-permute-start | bytes 36872 | tf_op jit(solution)/shard_map/ppermute | solution.py:14
  68.7 18.3 %psum.7 = f32[5,8,32]{2,1,0:T(8,128)S(1)} all-reduce(f32[5,8,32]{2,1,0:T(8,128)S(1)} %fusion.8), channel_id=1, replica_groups=mesh['grp'=2,'tile'=4,'sub'=4] {'tile'}, use_global_device_ids=true, to_apply=%region_1.2 | all-reduce | flops 1280 | bytes 10240 | tf_op jit(solution)/shard_map/psum | solution.py:154
  89.2 0.8 fusion.7
  (247 shorter events, 26.3 us)
Async XLA Ops:
  2.1 19.3 %collective-permute-start.12 = (f32[3,4,256]{2,0,1:T(4,128)S(1)}, f32[3,4,256]{2,0,1:T(4,128)S(1)}, u32[]{:S(2)}, u32[]{:S(2)}) collective-permute-start(f32[3,4,256]{2,0,1:T(4,128)S(1)} %constant_dynamic-update-slice_fusion.16), channel_id=1, source_target_pairs={{0,4},{4,8},{8,12},{12,0},{1,5},{5,9},{9,13},{13,1},{2,6},{6,10},{... | collective-permute-start | bytes 36872 | tf_op jit(solution)/shard_map/ppermute | solution.py:14
  5.2 19.0 %collective-permute-start.13 = (f32[3,4,256]{2,0,1:T(4,128)S(1)}, f32[3,4,256]{2,0,1:T(4,128)S(1)}, u32[]{:S(2)}, u32[]{:S(2)}) collective-permute-start(f32[3,4,256]{2,0,1:T(4,128)S(1)} %constant_dynamic-update-slice_fusion.16), channel_id=1, source_target_pairs={{0,8},{4,12},{8,0},{12,4},{1,9},{5,13},{9,1},{13,5},{2,10},{6,14},... | collective-permute-start | bytes 36872 | tf_op jit(solution)/shard_map/ppermute | solution.py:14
  7.8 16.4 %collective-permute-start.14 = (f32[3,4,256]{2,0,1:T(4,128)S(1)}, f32[3,4,256]{2,0,1:T(4,128)S(1)}, u32[]{:S(2)}, u32[]{:S(2)}) collective-permute-start(f32[3,4,256]{2,0,1:T(4,128)S(1)} %constant_dynamic-update-slice_fusion.16), channel_id=1, source_target_pairs={{0,12},{4,0},{8,4},{12,8},{1,13},{5,1},{9,5},{13,9},{2,14},{6,2},{... | collective-permute-start | bytes 36872 | tf_op jit(solution)/shard_map/ppermute | solution.py:14
  15.7 13.3 %collective-permute-start = (f32[3,4,256]{2,0,1:T(4,128)S(1)}, f32[3,4,256]{2,0,1:T(4,128)S(1)}, u32[]{:S(2)}, u32[]{:S(2)}) collective-permute-start(f32[3,4,256]{2,0,1:T(4,128)S(1)} %constant_dynamic-update-slice_fusion), channel_id=1, source_target_pairs={{0,4},{4,8},{8,12},{12,0},{1,5},{5,9},{9,13},{13,1},{2,6},{6,10},{... | collective-permute-start | bytes 36872 | tf_op jit(solution)/shard_map/ppermute | solution.py:14
  16.4 15.5 %collective-permute-start.1 = (f32[3,4,256]{2,0,1:T(4,128)S(1)}, f32[3,4,256]{2,0,1:T(4,128)S(1)}, u32[]{:S(2)}, u32[]{:S(2)}) collective-permute-start(f32[3,4,256]{2,0,1:T(4,128)S(1)} %constant_dynamic-update-slice_fusion), channel_id=1, source_target_pairs={{0,8},{4,12},{8,0},{12,4},{1,9},{5,13},{9,1},{13,5},{2,10},{6,14},... | collective-permute-start | bytes 36872 | tf_op jit(solution)/shard_map/ppermute | solution.py:14
  21.4 10.5 %collective-permute-start.2 = (f32[3,4,256]{2,0,1:T(4,128)S(1)}, f32[3,4,256]{2,0,1:T(4,128)S(1)}, u32[]{:S(2)}, u32[]{:S(2)}) collective-permute-start(f32[3,4,256]{2,0,1:T(4,128)S(1)} %constant_dynamic-update-slice_fusion), channel_id=1, source_target_pairs={{0,12},{4,0},{8,4},{12,8},{1,13},{5,1},{9,5},{13,9},{2,14},{6,2},{... | collective-permute-start | bytes 36872 | tf_op jit(solution)/shard_map/ppermute | solution.py:14
  26.7 9.2 %collective-permute-start.15 = (f32[3,4,256]{2,0,1:T(4,128)S(1)}, f32[3,4,256]{2,0,1:T(4,128)S(1)}, u32[]{:S(2)}, u32[]{:S(2)}) collective-permute-start(f32[3,4,256]{2,0,1:T(4,128)S(1)} %constant_dynamic-update-slice_fusion.20), channel_id=1, source_target_pairs={{0,4},{4,8},{8,12},{12,0},{1,5},{5,9},{9,13},{13,1},{2,6},{6,10},{... | collective-permute-start | bytes 36872 | tf_op jit(solution)/shard_map/ppermute | solution.py:14
  27.3 11.4 %collective-permute-start.16 = (f32[3,4,256]{2,0,1:T(4,128)S(1)}, f32[3,4,256]{2,0,1:T(4,128)S(1)}, u32[]{:S(2)}, u32[]{:S(2)}) collective-permute-start(f32[3,4,256]{2,0,1:T(4,128)S(1)} %constant_dynamic-update-slice_fusion.20), channel_id=1, source_target_pairs={{0,8},{4,12},{8,0},{12,4},{1,9},{5,13},{9,1},{13,5},{2,10},{6,14},... | collective-permute-start | bytes 36872 | tf_op jit(solution)/shard_map/ppermute | solution.py:14
  29.0 9.7 %collective-permute-start.17 = (f32[3,4,256]{2,0,1:T(4,128)S(1)}, f32[3,4,256]{2,0,1:T(4,128)S(1)}, u32[]{:S(2)}, u32[]{:S(2)}) collective-permute-start(f32[3,4,256]{2,0,1:T(4,128)S(1)} %constant_dynamic-update-slice_fusion.20), channel_id=1, source_target_pairs={{0,12},{4,0},{8,4},{12,8},{1,13},{5,1},{9,5},{13,9},{2,14},{6,2},{... | collective-permute-start | bytes 36872 | tf_op jit(solution)/shard_map/ppermute | solution.py:14
  34.3 9.1 %collective-permute-start.3 = (f32[3,4,256]{2,0,1:T(4,128)S(1)}, f32[3,4,256]{2,0,1:T(4,128)S(1)}, u32[]{:S(2)}, u32[]{:S(2)}) collective-permute-start(f32[3,4,256]{2,0,1:T(4,128)S(1)} %constant_dynamic-update-slice_fusion.4), channel_id=1, source_target_pairs={{0,4},{4,8},{8,12},{12,0},{1,5},{5,9},{9,13},{13,1},{2,6},{6,10},{... | collective-permute-start | bytes 36872 | tf_op jit(solution)/shard_map/ppermute | solution.py:14
  34.4 12.0 %collective-permute-start.4 = (f32[3,4,256]{2,0,1:T(4,128)S(1)}, f32[3,4,256]{2,0,1:T(4,128)S(1)}, u32[]{:S(2)}, u32[]{:S(2)}) collective-permute-start(f32[3,4,256]{2,0,1:T(4,128)S(1)} %constant_dynamic-update-slice_fusion.4), channel_id=1, source_target_pairs={{0,8},{4,12},{8,0},{12,4},{1,9},{5,13},{9,1},{13,5},{2,10},{6,14},... | collective-permute-start | bytes 36872 | tf_op jit(solution)/shard_map/ppermute | solution.py:14
  35.8 10.6 %collective-permute-start.5 = (f32[3,4,256]{2,0,1:T(4,128)S(1)}, f32[3,4,256]{2,0,1:T(4,128)S(1)}, u32[]{:S(2)}, u32[]{:S(2)}) collective-permute-start(f32[3,4,256]{2,0,1:T(4,128)S(1)} %constant_dynamic-update-slice_fusion.4), channel_id=1, source_target_pairs={{0,12},{4,0},{8,4},{12,8},{1,13},{5,1},{9,5},{13,9},{2,14},{6,2},{... | collective-permute-start | bytes 36872 | tf_op jit(solution)/shard_map/ppermute | solution.py:14
  41.2 9.2 %collective-permute-start.18 = (f32[3,4,256]{2,0,1:T(4,128)S(1)}, f32[3,4,256]{2,0,1:T(4,128)S(1)}, u32[]{:S(2)}, u32[]{:S(2)}) collective-permute-start(f32[3,4,256]{2,0,1:T(4,128)S(1)} %constant_dynamic-update-slice_fusion.24), channel_id=1, source_target_pairs={{0,4},{4,8},{8,12},{12,0},{1,5},{5,9},{9,13},{13,1},{2,6},{6,10},{... | collective-permute-start | bytes 36872 | tf_op jit(solution)/shard_map/ppermute | solution.py:14
  41.8 11.4 %collective-permute-start.19 = (f32[3,4,256]{2,0,1:T(4,128)S(1)}, f32[3,4,256]{2,0,1:T(4,128)S(1)}, u32[]{:S(2)}, u32[]{:S(2)}) collective-permute-start(f32[3,4,256]{2,0,1:T(4,128)S(1)} %constant_dynamic-update-slice_fusion.24), channel_id=1, source_target_pairs={{0,8},{4,12},{8,0},{12,4},{1,9},{5,13},{9,1},{13,5},{2,10},{6,14},... | collective-permute-start | bytes 36872 | tf_op jit(solution)/shard_map/ppermute | solution.py:14
  43.5 9.7 %collective-permute-start.20 = (f32[3,4,256]{2,0,1:T(4,128)S(1)}, f32[3,4,256]{2,0,1:T(4,128)S(1)}, u32[]{:S(2)}, u32[]{:S(2)}) collective-permute-start(f32[3,4,256]{2,0,1:T(4,128)S(1)} %constant_dynamic-update-slice_fusion.24), channel_id=1, source_target_pairs={{0,12},{4,0},{8,4},{12,8},{1,13},{5,1},{9,5},{13,9},{2,14},{6,2},{... | collective-permute-start | bytes 36872 | tf_op jit(solution)/shard_map/ppermute | solution.py:14
  48.8 9.1 %collective-permute-start.6 = (f32[3,4,256]{2,0,1:T(4,128)S(1)}, f32[3,4,256]{2,0,1:T(4,128)S(1)}, u32[]{:S(2)}, u32[]{:S(2)}) collective-permute-start(f32[3,4,256]{2,0,1:T(4,128)S(1)} %constant_dynamic-update-slice_fusion.8), channel_id=1, source_target_pairs={{0,4},{4,8},{8,12},{12,0},{1,5},{5,9},{9,13},{13,1},{2,6},{6,10},{... | collective-permute-start | bytes 36872 | tf_op jit(solution)/shard_map/ppermute | solution.py:14
  48.9 12.0 %collective-permute-start.7 = (f32[3,4,256]{2,0,1:T(4,128)S(1)}, f32[3,4,256]{2,0,1:T(4,128)S(1)}, u32[]{:S(2)}, u32[]{:S(2)}) collective-permute-start(f32[3,4,256]{2,0,1:T(4,128)S(1)} %constant_dynamic-update-slice_fusion.8), channel_id=1, source_target_pairs={{0,8},{4,12},{8,0},{12,4},{1,9},{5,13},{9,1},{13,5},{2,10},{6,14},... | collective-permute-start | bytes 36872 | tf_op jit(solution)/shard_map/ppermute | solution.py:14
  50.3 10.6 %collective-permute-start.8 = (f32[3,4,256]{2,0,1:T(4,128)S(1)}, f32[3,4,256]{2,0,1:T(4,128)S(1)}, u32[]{:S(2)}, u32[]{:S(2)}) collective-permute-start(f32[3,4,256]{2,0,1:T(4,128)S(1)} %constant_dynamic-update-slice_fusion.8), channel_id=1, source_target_pairs={{0,12},{4,0},{8,4},{12,8},{1,13},{5,1},{9,5},{13,9},{2,14},{6,2},{... | collective-permute-start | bytes 36872 | tf_op jit(solution)/shard_map/ppermute | solution.py:14
  55.7 10.0 %collective-permute-start.21 = (f32[3,4,256]{2,0,1:T(4,128)S(1)}, f32[3,4,256]{2,0,1:T(4,128)S(1)}, u32[]{:S(2)}, u32[]{:S(2)}) collective-permute-start(f32[3,4,256]{2,0,1:T(4,128)S(1)} %constant_dynamic-update-slice_fusion.28), channel_id=1, source_target_pairs={{0,4},{4,8},{8,12},{12,0},{1,5},{5,9},{9,13},{13,1},{2,6},{6,10},{... | collective-permute-start | bytes 36872 | tf_op jit(solution)/shard_map/ppermute | solution.py:14
  56.3 10.6 %collective-permute-start.22 = (f32[3,4,256]{2,0,1:T(4,128)S(1)}, f32[3,4,256]{2,0,1:T(4,128)S(1)}, u32[]{:S(2)}, u32[]{:S(2)}) collective-permute-start(f32[3,4,256]{2,0,1:T(4,128)S(1)} %constant_dynamic-update-slice_fusion.28), channel_id=1, source_target_pairs={{0,8},{4,12},{8,0},{12,4},{1,9},{5,13},{9,1},{13,5},{2,10},{6,14},... | collective-permute-start | bytes 36872 | tf_op jit(solution)/shard_map/ppermute | solution.py:14
  58.0 8.9 %collective-permute-start.23 = (f32[3,4,256]{2,0,1:T(4,128)S(1)}, f32[3,4,256]{2,0,1:T(4,128)S(1)}, u32[]{:S(2)}, u32[]{:S(2)}) collective-permute-start(f32[3,4,256]{2,0,1:T(4,128)S(1)} %constant_dynamic-update-slice_fusion.28), channel_id=1, source_target_pairs={{0,12},{4,0},{8,4},{12,8},{1,13},{5,1},{9,5},{13,9},{2,14},{6,2},{... | collective-permute-start | bytes 36872 | tf_op jit(solution)/shard_map/ppermute | solution.py:14
  63.3 24.3 %collective-permute-start.10 = (f32[3,4,256]{2,0,1:T(4,128)S(1)}, f32[3,4,256]{2,0,1:T(4,128)S(1)}, u32[]{:S(2)}, u32[]{:S(2)}) collective-permute-start(f32[3,4,256]{2,0,1:T(4,128)S(1)} %constant_dynamic-update-slice_fusion.12), channel_id=1, source_target_pairs={{0,8},{4,12},{8,0},{12,4},{1,9},{5,13},{9,1},{13,5},{2,10},{6,14},... | collective-permute-start | bytes 36872 | tf_op jit(solution)/shard_map/ppermute | solution.py:14
  64.3 23.3 %collective-permute-start.11 = (f32[3,4,256]{2,0,1:T(4,128)S(1)}, f32[3,4,256]{2,0,1:T(4,128)S(1)}, u32[]{:S(2)}, u32[]{:S(2)}) collective-permute-start(f32[3,4,256]{2,0,1:T(4,128)S(1)} %constant_dynamic-update-slice_fusion.12), channel_id=1, source_target_pairs={{0,12},{4,0},{8,4},{12,8},{1,13},{5,1},{9,5},{13,9},{2,14},{6,2},{... | collective-permute-start | bytes 36872 | tf_op jit(solution)/shard_map/ppermute | solution.py:14
  65.7 21.9 %collective-permute-start.9 = (f32[3,4,256]{2,0,1:T(4,128)S(1)}, f32[3,4,256]{2,0,1:T(4,128)S(1)}, u32[]{:S(2)}, u32[]{:S(2)}) collective-permute-start(f32[3,4,256]{2,0,1:T(4,128)S(1)} %constant_dynamic-update-slice_fusion.12), channel_id=1, source_target_pairs={{0,4},{4,8},{8,12},{12,0},{1,5},{5,9},{9,13},{13,1},{2,6},{6,10},{... | collective-permute-start | bytes 36872 | tf_op jit(solution)/shard_map/ppermute | solution.py:14
  (4 other events, 23.0 us)
where the time goes:
time: 90.1 us; the launch traced here: 89.9 us
  starting transfers between devices  36.9 us (41%)
  blocking collectives  23.9 us (27%)
  local copies, waits for them, and re-layouts  22.3 us (25%)
  matrix products  2.63 us (3%)
  other arithmetic  2.6 us (3%)
  between operations  1.55 us (2%)
    ppermute x24, starting transfers between devices, from_behind(): return lax.ppermute(value, axis, pairs)  36.9 us
    psum x1, blocking collectives, tile_total(): return lax.psum(filter_part, 'tile')  18.3 us
    all_gather x1, blocking collectives, on_device(): whole_grad = lax.all_gather(out_grad, 'sub', axis=1, tiled=True)  5.58 us
    gather x8, local copies, waits for them, and re-layouts, laplace(): ghosts = stacked[local_rows, my_edges]  4.87 us
    another operation x40, local copies, waits for them, and re-layouts, edge_lines(): jnp.stack([values[..., :tile_side], values[..., -tile_side:], values[...,...  2.57 us
  transfers between devices with their start and end apart: 24, of which 0 were waited for; matrix products, arithmetic and copies ran while one was open for 26% of the time, Pallas kernels for 0%

commit v1 on v0

--- a/solution.py
+++ b/solution.py
@@ -151,7 +151,12 @@
 
 
 def tile_total(filter_part):
-    return lax.psum(filter_part, "tile")
+
+    def connect_the_yards(xin, which_axis):
+        part_next = lax.all_gather(xin, which_axis)
+        return jnp.sum(part_next, axis=0)
+
+    return connect_the_yards(filter_part, "tile")
 
 
 def on_device(features, out_grad, filters, tile_map):

time: 90.1 us -> 85 us (0.943)
  blocking collectives: 23.9 us -> 18.8 us
    psum x1 -> x0, blocking collectives: 18.3 us -> none  [tile_total(): return lax.psum(filter_part, 'tile')]
    all_gather x0 -> x1, blocking collectives: none -> 13.2 us  [connect_the_yards(): part_next = lax.all_gather(xin, which_axis)]
  transfers between devices with their start and end apart: 24 -> 24, of which waited for: 0 -> 0; matrix products, arithmetic and copies ran while one was open for 26% -> 27% of each run, Pallas kernels for 0% -> 0%
where the time goes in v1:
time: 85 us; the launch traced here: 84.8 us
  starting transfers between devices  36.9 us (43%)
  local copies, waits for them, and re-layouts  22.3 us (26%)
  blocking collectives  18.8 us (22%)
  matrix products  2.63 us (3%)
  other arithmetic  2.61 us (3%)
  between operations  1.55 us (2%)
    ppermute x24, starting transfers between devices, from_behind(): return lax.ppermute(value, axis, pairs)  36.9 us
    all_gather x1, blocking collectives, connect_the_yards(): part_next = lax.all_gather(xin, which_axis)  13.2 us
    all_gather x1, blocking collectives, on_device(): whole_grad = lax.all_gather(out_grad, 'sub', axis=1, tiled=True)  5.58 us
    gather x8, local copies, waits for them, and re-layouts, laplace(): ghosts = stacked[local_rows, my_edges]  4.87 us
    another operation x40, local copies, waits for them, and re-layouts, edge_lines(): jnp.stack([values[..., :tile_side], values[..., -tile_side:], values[...,...  2.57 us
  transfers between devices with their start and end apart: 24, of which 0 were waited for; matrix products, arithmetic and copies ran while one was open for 27% of the time, Pallas kernels for 0%

profile of v1, /device:TPU:0, one launch (start us, length us, event | category | flops | bytes accessed | tf_op | source)
XLA Modules:
  0.0 84.8 jit_solution(2871885318123559040)
XLA Ops:
  0.7 0.8 fusion.100
  2.1 3.1 %collective-permute-start.12 = (f32[3,4,256]{2,0,1:T(4,128)S(1)}, f32[3,4,256]{2,0,1:T(4,128)S(1)}, u32[]{:S(2)}, u32[]{:S(2)}) collective-permute-start(f32[3,4,256]{2,0,1:T(4,128)S(1)} %constant_dynamic-update-slice_fusion.16), channel_id=1, source_target_pairs={{0,4},{4,8},{8,12},{12,0},{1,5},{5,9},{9,13},{13,1},{2,6},{6,10},{... | collective-permute-start | bytes 36872 | tf_op jit(solution)/shard_map/ppermute | solution.py:14
  5.2 2.6 %collective-permute-start.13 = (f32[3,4,256]{2,0,1:T(4,128)S(1)}, f32[3,4,256]{2,0,1:T(4,128)S(1)}, u32[]{:S(2)}, u32[]{:S(2)}) collective-permute-start(f32[3,4,256]{2,0,1:T(4,128)S(1)} %constant_dynamic-update-slice_fusion.16), channel_id=1, source_target_pairs={{0,8},{4,12},{8,0},{12,4},{1,9},{5,13},{9,1},{13,5},{2,10},{6,14},... | collective-permute-start | bytes 36872 | tf_op jit(solution)/shard_map/ppermute | solution.py:14
  7.8 1.3 %collective-permute-start.14 = (f32[3,4,256]{2,0,1:T(4,128)S(1)}, f32[3,4,256]{2,0,1:T(4,128)S(1)}, u32[]{:S(2)}, u32[]{:S(2)}) collective-permute-start(f32[3,4,256]{2,0,1:T(4,128)S(1)} %constant_dynamic-update-slice_fusion.16), channel_id=1, source_target_pairs={{0,12},{4,0},{8,4},{12,8},{1,13},{5,1},{9,5},{13,9},{2,14},{6,2},{... | collective-permute-start | bytes 36872 | tf_op jit(solution)/shard_map/ppermute | solution.py:14
  9.2 5.6 %all_gather.9 = bf16[3,32,1024]{2,1,0:T(8,128)(2,1)S(1)} all-gather(bf16[3,8,1024]{2,1,0:T(8,128)(2,1)S(1)} %copy-done.2), channel_id=1, replica_groups=mesh['grp'=2,'tile'=4,'sub'=4] {'sub'}, dimensions={1}, use_global_device_ids=true | all-gather | bytes 245760 | tf_op jit(solution)/shard_map/all_gather | solution.py:192
  15.7 0.7 collective-permute-start
  18.3 1.2 %sort.17 = (s32[12]{0:T(128)}, s32[12]{0:T(128)S(1)}) sort(s32[12]{0:T(128)S(1)} %copy-done.3, s32[12]{0:T(128)S(1)} %iota.45), dimensions={0}, to_apply=%region_0.1 | sort | flops 48 | bytes 192 | tf_op jit(solution)/shard_map/jit(argsort)/sort | solution.py:107
  19.5 0.8 gather_fusion
  21.4 2.8 %collective-permute-start.2 = (f32[3,4,256]{2,0,1:T(4,128)S(1)}, f32[3,4,256]{2,0,1:T(4,128)S(1)}, u32[]{:S(2)}, u32[]{:S(2)}) collective-permute-start(f32[3,4,256]{2,0,1:T(4,128)S(1)} %constant_dynamic-update-slice_fusion), channel_id=1, source_target_pairs={{0,12},{4,0},{8,4},{12,8},{1,13},{5,1},{9,5},{13,9},{2,14},{6,2},{... | collective-permute-start | bytes 36872 | tf_op jit(solution)/shard_map/ppermute | solution.py:14
  27.3 1.5 %collective-permute-start.16 = (f32[3,4,256]{2,0,1:T(4,128)S(1)}, f32[3,4,256]{2,0,1:T(4,128)S(1)}, u32[]{:S(2)}, u32[]{:S(2)}) collective-permute-start(f32[3,4,256]{2,0,1:T(4,128)S(1)} %constant_dynamic-update-slice_fusion.20), channel_id=1, source_target_pairs={{0,8},{4,12},{8,0},{12,4},{1,9},{5,13},{9,1},{13,5},{2,10},{6,14},... | collective-permute-start | bytes 36872 | tf_op jit(solution)/shard_map/ppermute | solution.py:14
  29.0 2.9 %collective-permute-start.17 = (f32[3,4,256]{2,0,1:T(4,128)S(1)}, f32[3,4,256]{2,0,1:T(4,128)S(1)}, u32[]{:S(2)}, u32[]{:S(2)}) collective-permute-start(f32[3,4,256]{2,0,1:T(4,128)S(1)} %constant_dynamic-update-slice_fusion.20), channel_id=1, source_target_pairs={{0,12},{4,0},{8,4},{12,8},{1,13},{5,1},{9,5},{13,9},{2,14},{6,2},{... | collective-permute-start | bytes 36872 | tf_op jit(solution)/shard_map/ppermute | solution.py:14
  34.4 1.0 %collective-permute-start.4 = (f32[3,4,256]{2,0,1:T(4,128)S(1)}, f32[3,4,256]{2,0,1:T(4,128)S(1)}, u32[]{:S(2)}, u32[]{:S(2)}) collective-permute-start(f32[3,4,256]{2,0,1:T(4,128)S(1)} %constant_dynamic-update-slice_fusion.4), channel_id=1, source_target_pairs={{0,8},{4,12},{8,0},{12,4},{1,9},{5,13},{9,1},{13,5},{2,10},{6,14},... | collective-permute-start | bytes 36872 | tf_op jit(solution)/shard_map/ppermute | solution.py:14
  35.8 2.9 %collective-permute-start.5 = (f32[3,4,256]{2,0,1:T(4,128)S(1)}, f32[3,4,256]{2,0,1:T(4,128)S(1)}, u32[]{:S(2)}, u32[]{:S(2)}) collective-permute-start(f32[3,4,256]{2,0,1:T(4,128)S(1)} %constant_dynamic-update-slice_fusion.4), channel_id=1, source_target_pairs={{0,12},{4,0},{8,4},{12,8},{1,13},{5,1},{9,5},{13,9},{2,14},{6,2},{... | collective-permute-start | bytes 36872 | tf_op jit(solution)/shard_map/ppermute | solution.py:14
  41.8 1.5 %collective-permute-start.19 = (f32[3,4,256]{2,0,1:T(4,128)S(1)}, f32[3,4,256]{2,0,1:T(4,128)S(1)}, u32[]{:S(2)}, u32[]{:S(2)}) collective-permute-start(f32[3,4,256]{2,0,1:T(4,128)S(1)} %constant_dynamic-update-slice_fusion.24), channel_id=1, source_target_pairs={{0,8},{4,12},{8,0},{12,4},{1,9},{5,13},{9,1},{13,5},{2,10},{6,14},... | collective-permute-start | bytes 36872 | tf_op jit(solution)/shard_map/ppermute | solution.py:14
  43.5 2.9 %collective-permute-start.20 = (f32[3,4,256]{2,0,1:T(4,128)S(1)}, f32[3,4,256]{2,0,1:T(4,128)S(1)}, u32[]{:S(2)}, u32[]{:S(2)}) collective-permute-start(f32[3,4,256]{2,0,1:T(4,128)S(1)} %constant_dynamic-update-slice_fusion.24), channel_id=1, source_target_pairs={{0,12},{4,0},{8,4},{12,8},{1,13},{5,1},{9,5},{13,9},{2,14},{6,2},{... | collective-permute-start | bytes 36872 | tf_op jit(solution)/shard_map/ppermute | solution.py:14
  48.9 1.0 %collective-permute-start.7 = (f32[3,4,256]{2,0,1:T(4,128)S(1)}, f32[3,4,256]{2,0,1:T(4,128)S(1)}, u32[]{:S(2)}, u32[]{:S(2)}) collective-permute-start(f32[3,4,256]{2,0,1:T(4,128)S(1)} %constant_dynamic-update-slice_fusion.8), channel_id=1, source_target_pairs={{0,8},{4,12},{8,0},{12,4},{1,9},{5,13},{9,1},{13,5},{2,10},{6,14},... | collective-permute-start | bytes 36872 | tf_op jit(solution)/shard_map/ppermute | solution.py:14
  50.3 2.9 %collective-permute-start.8 = (f32[3,4,256]{2,0,1:T(4,128)S(1)}, f32[3,4,256]{2,0,1:T(4,128)S(1)}, u32[]{:S(2)}, u32[]{:S(2)}) collective-permute-start(f32[3,4,256]{2,0,1:T(4,128)S(1)} %constant_dynamic-update-slice_fusion.8), channel_id=1, source_target_pairs={{0,12},{4,0},{8,4},{12,8},{1,13},{5,1},{9,5},{13,9},{2,14},{6,2},{... | collective-permute-start | bytes 36872 | tf_op jit(solution)/shard_map/ppermute | solution.py:14
  56.3 1.5 %collective-permute-start.22 = (f32[3,4,256]{2,0,1:T(4,128)S(1)}, f32[3,4,256]{2,0,1:T(4,128)S(1)}, u32[]{:S(2)}, u32[]{:S(2)}) collective-permute-start(f32[3,4,256]{2,0,1:T(4,128)S(1)} %constant_dynamic-update-slice_fusion.28), channel_id=1, source_target_pairs={{0,8},{4,12},{8,0},{12,4},{1,9},{5,13},{9,1},{13,5},{2,10},{6,14},... | collective-permute-start | bytes 36872 | tf_op jit(solution)/shard_map/ppermute | solution.py:14
  58.0 2.9 %collective-permute-start.23 = (f32[3,4,256]{2,0,1:T(4,128)S(1)}, f32[3,4,256]{2,0,1:T(4,128)S(1)}, u32[]{:S(2)}, u32[]{:S(2)}) collective-permute-start(f32[3,4,256]{2,0,1:T(4,128)S(1)} %constant_dynamic-update-slice_fusion.28), channel_id=1, source_target_pairs={{0,12},{4,0},{8,4},{12,8},{1,13},{5,1},{9,5},{13,9},{2,14},{6,2},{... | collective-permute-start | bytes 36872 | tf_op jit(solution)/shard_map/ppermute | solution.py:14
  63.3 1.0 %collective-permute-start.10 = (f32[3,4,256]{2,0,1:T(4,128)S(1)}, f32[3,4,256]{2,0,1:T(4,128)S(1)}, u32[]{:S(2)}, u32[]{:S(2)}) collective-permute-start(f32[3,4,256]{2,0,1:T(4,128)S(1)} %constant_dynamic-update-slice_fusion.12), channel_id=1, source_target_pairs={{0,8},{4,12},{8,0},{12,4},{1,9},{5,13},{9,1},{13,5},{2,10},{6,14},... | collective-permute-start | bytes 36872 | tf_op jit(solution)/shard_map/ppermute | solution.py:14
  64.3 0.9 %collective-permute-start.11 = (f32[3,4,256]{2,0,1:T(4,128)S(1)}, f32[3,4,256]{2,0,1:T(4,128)S(1)}, u32[]{:S(2)}, u32[]{:S(2)}) collective-permute-start(f32[3,4,256]{2,0,1:T(4,128)S(1)} %constant_dynamic-update-slice_fusion.12), channel_id=1, source_target_pairs={{0,12},{4,0},{8,4},{12,8},{1,13},{5,1},{9,5},{13,9},{2,14},{6,2},{... | collective-permute-start | bytes 36872 | tf_op jit(solution)/shard_map/ppermute | solution.py:14
  65.7 1.1 %collective-permute-start.9 = (f32[3,4,256]{2,0,1:T(4,128)S(1)}, f32[3,4,256]{2,0,1:T(4,128)S(1)}, u32[]{:S(2)}, u32[]{:S(2)}) collective-permute-start(f32[3,4,256]{2,0,1:T(4,128)S(1)} %constant_dynamic-update-slice_fusion.12), channel_id=1, source_target_pairs={{0,4},{4,8},{8,12},{12,0},{1,5},{5,9},{9,13},{13,1},{2,6},{6,10},{... | collective-permute-start | bytes 36872 | tf_op jit(solution)/shard_map/ppermute | solution.py:14
  68.7 13.2 %all-gather = f32[20,8,32]{2,1,0:T(8,128)S(1)} all-gather(f32[5,8,32]{2,1,0:T(8,128)S(1)} %fusion.8), channel_id=2, replica_groups=mesh['grp'=2,'tile'=4,'sub'=4] {'tile'}, dimensions={0}, use_global_device_ids=true | all-gather | bytes 25600 | tf_op jit(solution)/shard_map/all_gather | solution.py:156
  84.0 0.8 fusion.7
  (248 shorter events, 26.3 us)
Async XLA Ops:
  2.1 19.3 %collective-permute-start.12 = (f32[3,4,256]{2,0,1:T(4,128)S(1)}, f32[3,4,256]{2,0,1:T(4,128)S(1)}, u32[]{:S(2)}, u32[]{:S(2)}) collective-permute-start(f32[3,4,256]{2,0,1:T(4,128)S(1)} %constant_dynamic-update-slice_fusion.16), channel_id=1, source_target_pairs={{0,4},{4,8},{8,12},{12,0},{1,5},{5,9},{9,13},{13,1},{2,6},{6,10},{... | collective-permute-start | bytes 36872 | tf_op jit(solution)/shard_map/ppermute | solution.py:14
  5.2 19.0 %collective-permute-start.13 = (f32[3,4,256]{2,0,1:T(4,128)S(1)}, f32[3,4,256]{2,0,1:T(4,128)S(1)}, u32[]{:S(2)}, u32[]{:S(2)}) collective-permute-start(f32[3,4,256]{2,0,1:T(4,128)S(1)} %constant_dynamic-update-slice_fusion.16), channel_id=1, source_target_pairs={{0,8},{4,12},{8,0},{12,4},{1,9},{5,13},{9,1},{13,5},{2,10},{6,14},... | collective-permute-start | bytes 36872 | tf_op jit(solution)/shard_map/ppermute | solution.py:14
  7.8 16.4 %collective-permute-start.14 = (f32[3,4,256]{2,0,1:T(4,128)S(1)}, f32[3,4,256]{2,0,1:T(4,128)S(1)}, u32[]{:S(2)}, u32[]{:S(2)}) collective-permute-start(f32[3,4,256]{2,0,1:T(4,128)S(1)} %constant_dynamic-update-slice_fusion.16), channel_id=1, source_target_pairs={{0,12},{4,0},{8,4},{12,8},{1,13},{5,1},{9,5},{13,9},{2,14},{6,2},{... | collective-permute-start | bytes 36872 | tf_op jit(solution)/shard_map/ppermute | solution.py:14
  15.7 13.3 %collective-permute-start = (f32[3,4,256]{2,0,1:T(4,128)S(1)}, f32[3,4,256]{2,0,1:T(4,128)S(1)}, u32[]{:S(2)}, u32[]{:S(2)}) collective-permute-start(f32[3,4,256]{2,0,1:T(4,128)S(1)} %constant_dynamic-update-slice_fusion), channel_id=1, source_target_pairs={{0,4},{4,8},{8,12},{12,0},{1,5},{5,9},{9,13},{13,1},{2,6},{6,10},{... | collective-permute-start | bytes 36872 | tf_op jit(solution)/shard_map/ppermute | solution.py:14
  16.4 15.5 %collective-permute-start.1 = (f32[3,4,256]{2,0,1:T(4,128)S(1)}, f32[3,4,256]{2,0,1:T(4,128)S(1)}, u32[]{:S(2)}, u32[]{:S(2)}) collective-permute-start(f32[3,4,256]{2,0,1:T(4,128)S(1)} %constant_dynamic-update-slice_fusion), channel_id=1, source_target_pairs={{0,8},{4,12},{8,0},{12,4},{1,9},{5,13},{9,1},{13,5},{2,10},{6,14},... | collective-permute-start | bytes 36872 | tf_op jit(solution)/shard_map/ppermute | solution.py:14
  21.4 10.5 %collective-permute-start.2 = (f32[3,4,256]{2,0,1:T(4,128)S(1)}, f32[3,4,256]{2,0,1:T(4,128)S(1)}, u32[]{:S(2)}, u32[]{:S(2)}) collective-permute-start(f32[3,4,256]{2,0,1:T(4,128)S(1)} %constant_dynamic-update-slice_fusion), channel_id=1, source_target_pairs={{0,12},{4,0},{8,4},{12,8},{1,13},{5,1},{9,5},{13,9},{2,14},{6,2},{... | collective-permute-start | bytes 36872 | tf_op jit(solution)/shard_map/ppermute | solution.py:14
  26.7 9.2 %collective-permute-start.15 = (f32[3,4,256]{2,0,1:T(4,128)S(1)}, f32[3,4,256]{2,0,1:T(4,128)S(1)}, u32[]{:S(2)}, u32[]{:S(2)}) collective-permute-start(f32[3,4,256]{2,0,1:T(4,128)S(1)} %constant_dynamic-update-slice_fusion.20), channel_id=1, source_target_pairs={{0,4},{4,8},{8,12},{12,0},{1,5},{5,9},{9,13},{13,1},{2,6},{6,10},{... | collective-permute-start | bytes 36872 | tf_op jit(solution)/shard_map/ppermute | solution.py:14
  27.3 11.4 %collective-permute-start.16 = (f32[3,4,256]{2,0,1:T(4,128)S(1)}, f32[3,4,256]{2,0,1:T(4,128)S(1)}, u32[]{:S(2)}, u32[]{:S(2)}) collective-permute-start(f32[3,4,256]{2,0,1:T(4,128)S(1)} %constant_dynamic-update-slice_fusion.20), channel_id=1, source_target_pairs={{0,8},{4,12},{8,0},{12,4},{1,9},{5,13},{9,1},{13,5},{2,10},{6,14},... | collective-permute-start | bytes 36872 | tf_op jit(solution)/shard_map/ppermute | solution.py:14
  29.0 9.7 %collective-permute-start.17 = (f32[3,4,256]{2,0,1:T(4,128)S(1)}, f32[3,4,256]{2,0,1:T(4,128)S(1)}, u32[]{:S(2)}, u32[]{:S(2)}) collective-permute-start(f32[3,4,256]{2,0,1:T(4,128)S(1)} %constant_dynamic-update-slice_fusion.20), channel_id=1, source_target_pairs={{0,12},{4,0},{8,4},{12,8},{1,13},{5,1},{9,5},{13,9},{2,14},{6,2},{... | collective-permute-start | bytes 36872 | tf_op jit(solution)/shard_map/ppermute | solution.py:14
  34.3 9.1 %collective-permute-start.3 = (f32[3,4,256]{2,0,1:T(4,128)S(1)}, f32[3,4,256]{2,0,1:T(4,128)S(1)}, u32[]{:S(2)}, u32[]{:S(2)}) collective-permute-start(f32[3,4,256]{2,0,1:T(4,128)S(1)} %constant_dynamic-update-slice_fusion.4), channel_id=1, source_target_pairs={{0,4},{4,8},{8,12},{12,0},{1,5},{5,9},{9,13},{13,1},{2,6},{6,10},{... | collective-permute-start | bytes 36872 | tf_op jit(solution)/shard_map/ppermute | solution.py:14
  34.4 12.0 %collective-permute-start.4 = (f32[3,4,256]{2,0,1:T(4,128)S(1)}, f32[3,4,256]{2,0,1:T(4,128)S(1)}, u32[]{:S(2)}, u32[]{:S(2)}) collective-permute-start(f32[3,4,256]{2,0,1:T(4,128)S(1)} %constant_dynamic-update-slice_fusion.4), channel_id=1, source_target_pairs={{0,8},{4,12},{8,0},{12,4},{1,9},{5,13},{9,1},{13,5},{2,10},{6,14},... | collective-permute-start | bytes 36872 | tf_op jit(solution)/shard_map/ppermute | solution.py:14
  35.8 10.6 %collective-permute-start.5 = (f32[3,4,256]{2,0,1:T(4,128)S(1)}, f32[3,4,256]{2,0,1:T(4,128)S(1)}, u32[]{:S(2)}, u32[]{:S(2)}) collective-permute-start(f32[3,4,256]{2,0,1:T(4,128)S(1)} %constant_dynamic-update-slice_fusion.4), channel_id=1, source_target_pairs={{0,12},{4,0},{8,4},{12,8},{1,13},{5,1},{9,5},{13,9},{2,14},{6,2},{... | collective-permute-start | bytes 36872 | tf_op jit(solution)/shard_map/ppermute | solution.py:14
  41.2 9.2 %collective-permute-start.18 = (f32[3,4,256]{2,0,1:T(4,128)S(1)}, f32[3,4,256]{2,0,1:T(4,128)S(1)}, u32[]{:S(2)}, u32[]{:S(2)}) collective-permute-start(f32[3,4,256]{2,0,1:T(4,128)S(1)} %constant_dynamic-update-slice_fusion.24), channel_id=1, source_target_pairs={{0,4},{4,8},{8,12},{12,0},{1,5},{5,9},{9,13},{13,1},{2,6},{6,10},{... | collective-permute-start | bytes 36872 | tf_op jit(solution)/shard_map/ppermute | solution.py:14
  41.8 11.4 %collective-permute-start.19 = (f32[3,4,256]{2,0,1:T(4,128)S(1)}, f32[3,4,256]{2,0,1:T(4,128)S(1)}, u32[]{:S(2)}, u32[]{:S(2)}) collective-permute-start(f32[3,4,256]{2,0,1:T(4,128)S(1)} %constant_dynamic-update-slice_fusion.24), channel_id=1, source_target_pairs={{0,8},{4,12},{8,0},{12,4},{1,9},{5,13},{9,1},{13,5},{2,10},{6,14},... | collective-permute-start | bytes 36872 | tf_op jit(solution)/shard_map/ppermute | solution.py:14
  43.5 9.7 %collective-permute-start.20 = (f32[3,4,256]{2,0,1:T(4,128)S(1)}, f32[3,4,256]{2,0,1:T(4,128)S(1)}, u32[]{:S(2)}, u32[]{:S(2)}) collective-permute-start(f32[3,4,256]{2,0,1:T(4,128)S(1)} %constant_dynamic-update-slice_fusion.24), channel_id=1, source_target_pairs={{0,12},{4,0},{8,4},{12,8},{1,13},{5,1},{9,5},{13,9},{2,14},{6,2},{... | collective-permute-start | bytes 36872 | tf_op jit(solution)/shard_map/ppermute | solution.py:14
  48.8 9.1 %collective-permute-start.6 = (f32[3,4,256]{2,0,1:T(4,128)S(1)}, f32[3,4,256]{2,0,1:T(4,128)S(1)}, u32[]{:S(2)}, u32[]{:S(2)}) collective-permute-start(f32[3,4,256]{2,0,1:T(4,128)S(1)} %constant_dynamic-update-slice_fusion.8), channel_id=1, source_target_pairs={{0,4},{4,8},{8,12},{12,0},{1,5},{5,9},{9,13},{13,1},{2,6},{6,10},{... | collective-permute-start | bytes 36872 | tf_op jit(solution)/shard_map/ppermute | solution.py:14
  48.9 12.0 %collective-permute-start.7 = (f32[3,4,256]{2,0,1:T(4,128)S(1)}, f32[3,4,256]{2,0,1:T(4,128)S(1)}, u32[]{:S(2)}, u32[]{:S(2)}) collective-permute-start(f32[3,4,256]{2,0,1:T(4,128)S(1)} %constant_dynamic-update-slice_fusion.8), channel_id=1, source_target_pairs={{0,8},{4,12},{8,0},{12,4},{1,9},{5,13},{9,1},{13,5},{2,10},{6,14},... | collective-permute-start | bytes 36872 | tf_op jit(solution)/shard_map/ppermute | solution.py:14
  50.3 10.6 %collective-permute-start.8 = (f32[3,4,256]{2,0,1:T(4,128)S(1)}, f32[3,4,256]{2,0,1:T(4,128)S(1)}, u32[]{:S(2)}, u32[]{:S(2)}) collective-permute-start(f32[3,4,256]{2,0,1:T(4,128)S(1)} %constant_dynamic-update-slice_fusion.8), channel_id=1, source_target_pairs={{0,12},{4,0},{8,4},{12,8},{1,13},{5,1},{9,5},{13,9},{2,14},{6,2},{... | collective-permute-start | bytes 36872 | tf_op jit(solution)/shard_map/ppermute | solution.py:14
  55.7 10.0 %collective-permute-start.21 = (f32[3,4,256]{2,0,1:T(4,128)S(1)}, f32[3,4,256]{2,0,1:T(4,128)S(1)}, u32[]{:S(2)}, u32[]{:S(2)}) collective-permute-start(f32[3,4,256]{2,0,1:T(4,128)S(1)} %constant_dynamic-update-slice_fusion.28), channel_id=1, source_target_pairs={{0,4},{4,8},{8,12},{12,0},{1,5},{5,9},{9,13},{13,1},{2,6},{6,10},{... | collective-permute-start | bytes 36872 | tf_op jit(solution)/shard_map/ppermute | solution.py:14
  56.3 10.6 %collective-permute-start.22 = (f32[3,4,256]{2,0,1:T(4,128)S(1)}, f32[3,4,256]{2,0,1:T(4,128)S(1)}, u32[]{:S(2)}, u32[]{:S(2)}) collective-permute-start(f32[3,4,256]{2,0,1:T(4,128)S(1)} %constant_dynamic-update-slice_fusion.28), channel_id=1, source_target_pairs={{0,8},{4,12},{8,0},{12,4},{1,9},{5,13},{9,1},{13,5},{2,10},{6,14},... | collective-permute-start | bytes 36872 | tf_op jit(solution)/shard_map/ppermute | solution.py:14
  58.0 8.9 %collective-permute-start.23 = (f32[3,4,256]{2,0,1:T(4,128)S(1)}, f32[3,4,256]{2,0,1:T(4,128)S(1)}, u32[]{:S(2)}, u32[]{:S(2)}) collective-permute-start(f32[3,4,256]{2,0,1:T(4,128)S(1)} %constant_dynamic-update-slice_fusion.28), channel_id=1, source_target_pairs={{0,12},{4,0},{8,4},{12,8},{1,13},{5,1},{9,5},{13,9},{2,14},{6,2},{... | collective-permute-start | bytes 36872 | tf_op jit(solution)/shard_map/ppermute | solution.py:14
  63.3 19.2 %collective-permute-start.10 = (f32[3,4,256]{2,0,1:T(4,128)S(1)}, f32[3,4,256]{2,0,1:T(4,128)S(1)}, u32[]{:S(2)}, u32[]{:S(2)}) collective-permute-start(f32[3,4,256]{2,0,1:T(4,128)S(1)} %constant_dynamic-update-slice_fusion.12), channel_id=1, source_target_pairs={{0,8},{4,12},{8,0},{12,4},{1,9},{5,13},{9,1},{13,5},{2,10},{6,14},... | collective-permute-start | bytes 36872 | tf_op jit(solution)/shard_map/ppermute | solution.py:14
  64.3 18.2 %collective-permute-start.11 = (f32[3,4,256]{2,0,1:T(4,128)S(1)}, f32[3,4,256]{2,0,1:T(4,128)S(1)}, u32[]{:S(2)}, u32[]{:S(2)}) collective-permute-start(f32[3,4,256]{2,0,1:T(4,128)S(1)} %constant_dynamic-update-slice_fusion.12), channel_id=1, source_target_pairs={{0,12},{4,0},{8,4},{12,8},{1,13},{5,1},{9,5},{13,9},{2,14},{6,2},{... | collective-permute-start | bytes 36872 | tf_op jit(solution)/shard_map/ppermute | solution.py:14
  65.7 16.8 %collective-permute-start.9 = (f32[3,4,256]{2,0,1:T(4,128)S(1)}, f32[3,4,256]{2,0,1:T(4,128)S(1)}, u32[]{:S(2)}, u32[]{:S(2)}) collective-permute-start(f32[3,4,256]{2,0,1:T(4,128)S(1)} %constant_dynamic-update-slice_fusion.12), channel_id=1, source_target_pairs={{0,4},{4,8},{8,12},{12,0},{1,5},{5,9},{9,13},{13,1},{2,6},{6,10},{... | collective-permute-start | bytes 36872 | tf_op jit(solution)/shard_map/ppermute | solution.py:14
  (4 other events, 23.0 us)
